TPU v7x, 32 devices: a whole 2x2x4 slice. The times are simulated.
32 devices in a mesh: fsdp: 8 (over y, x, core), tp: 4 (over z).
Axes of the slice: x: 2, y: 2, z: 4, core: 2. Of those that a mesh axis runs over, the one named last changes fastest.
Arguments:
- block_in: bfloat16 [16, 1024, 3072], P('fsdp', 'tp'), may hold values from -6 to 6
- out_cotangent: bfloat16 [16, 1024, 3072], P('fsdp', 'tp'), may hold values from -6 to 6
- segment_ids: int32 [16, 1024], P('fsdp', 'tp'), may hold values from 0 to 3, as said below
- doc_positions: int32 [16, 1024], P('fsdp', 'tp'), may hold values from 0 to 799, as said below
- norm1_gain: bfloat16 [3072], replicated, may hold values from 0.5 to 1.5
- qkv_weight: bfloat16 [3072, 3, 3072], P('fsdp', None, 'tp'), may hold values from -0.5 to 0.5
- out_weight: bfloat16 [3072, 3072], P(('tp', 'fsdp')), may hold values from -0.875 to 0.875
- norm2_gain: bfloat16 [3072], replicated, may hold values from 0.5 to 1.5
- gate_up_weight: bfloat16 [3072, 2, 8192], P('fsdp', None, 'tp'), may hold values from -0.109375 to 0.109375
- down_weight: bfloat16 [8192, 3072], P(('tp', 'fsdp')), may hold values from -0.0625 to 0.0625
Outputs:
- block_out: bfloat16 [16, 1024, 3072], P('fsdp', 'tp')
- in_grad: float32 [16, 1024, 3072], P('fsdp', 'tp')
- norm1_gain_grad: float32 [3072], P(('fsdp', 'tp'))
- qkv_weight_grad: float32 [3072, 3, 3072], P('fsdp', None, 'tp')
- out_weight_grad: float32 [3072, 3072], P(('tp', 'fsdp'))
- norm2_gain_grad: float32 [3072], P(('fsdp', 'tp'))
- gate_up_weight_grad: float32 [3072, 2, 8192], P('fsdp', None, 'tp')
- down_weight_grad: float32 [8192, 3072], P(('tp', 'fsdp'))
Inputs may be any that keep to these rules, and one draw needn't show every extreme that they name: `segment_ids`: within each sequence the numbers start at 0, never fall and rise by at most one from a token to the next; every document has 60 to 800 tokens, and the first document of each sequence has 800. `doc_positions`: 0 at the first token of each document, else one more than at the token before.
All inputs are finite; a program needn't handle non-finite values.
Results may differ from a plain program's by a relative error of at most 0.017.
Values may be sent and summed in bfloat16 or wider, within the bound.
A program may use at most 256 MiB of HBM per device.

v0:
```python
import jax
import jax.numpy as jnp
from jax import lax
from jax.sharding import PartitionSpec as P

D = 3072
HD = 96
rms_epsilon = 1e-05
rope_theta = 10000.0
masked_score = -1e30


def rope_tables(positions, head_size):
    half_width = head_size // 2
    frequency = rope_theta ** (-(jnp.arange(half_width, dtype=jnp.float32) * 2.0 / head_size))
    angles = positions.astype(jnp.float32)[:, None] * frequency[None, :]
    return (jnp.cos(angles)[:, None, :], jnp.sin(angles)[:, None, :])


def rotate(values, cosine_part, sine_part):
    half_width = values.shape[-1] // 2
    lead_half = values[..., :half_width]
    tail_half = values[..., half_width:]
    return jnp.concatenate(
        [
            lead_half * cosine_part - tail_half * sine_part,
            tail_half * cosine_part + lead_half * sine_part,
        ],
        axis=-1,
    )


def unrotate(values, cosine_part, sine_part):
    half_width = values.shape[-1] // 2
    lead_half = values[..., :half_width]
    tail_half = values[..., half_width:]
    return jnp.concatenate(
        [
            lead_half * cosine_part + tail_half * sine_part,
            tail_half * cosine_part - lead_half * sine_part,
        ],
        axis=-1,
    )


def rms_scale(stream):
    return lax.rsqrt(jnp.mean(stream * stream, axis=-1, keepdims=True) + rms_epsilon)


def norm_back(stream, scale_rows, gain_vec, grad_rows):
    gained_grad = gain_vec * grad_rows
    input_grad = scale_rows * gained_grad - stream * scale_rows**3 * jnp.mean(
        gained_grad * stream, axis=-1, keepdims=True
    )
    return (input_grad, jnp.sum(grad_rows * stream * scale_rows, axis=0))


def allowed_mask(segment_tile, index_tile, segments):
    columns = jnp.arange(segments.shape[0], dtype=jnp.int32)
    return (segment_tile[:, None] == segments[None, :]) & (index_tile[:, None] >= columns[None, :])


def masked_scores(query_tile, key_rows, segment_tile, index_tile, segments, scale_value):
    scores = (
        jnp.einsum("qhd,khd->hqk", query_tile, key_rows, preferred_element_type=jnp.float32)
        * scale_value
    )
    return jnp.where(allowed_mask(segment_tile, index_tile, segments)[None], scores, masked_score)


def attention_forward(queries, key_rows, value_rows, segments, block_rows):
    seq_len, head_count, head_size = queries.shape
    tiles = seq_len // block_rows
    scale_value = head_size ** (-0.5)
    positions = jnp.arange(seq_len, dtype=jnp.int32)

    def query_block(packed):
        query_tile, segment_tile, index_tile = packed
        scores = masked_scores(
            query_tile, key_rows, segment_tile, index_tile, segments, scale_value
        )
        row_max = jnp.max(scores, axis=-1, keepdims=True)
        exponent = jnp.exp(scores - row_max)
        row_total = jnp.sum(exponent, axis=-1, keepdims=True)
        probs_low = (exponent / row_total).astype(jnp.bfloat16)
        mixed = jnp.einsum(
            "hqk,khd->qhd", probs_low, value_rows, preferred_element_type=jnp.float32
        )
        return (mixed, (row_max + jnp.log(row_total))[..., 0])

    mixed, log_total = lax.map(
        query_block,
        (
            queries.reshape(tiles, block_rows, head_count, head_size),
            segments.reshape(tiles, block_rows),
            positions.reshape(tiles, block_rows),
        ),
    )
    return (mixed.reshape(seq_len, head_count * head_size), log_total)


def attention_backward(queries, key_rows, value_rows, segments, log_total, out_grad, block_rows):
    seq_len, head_count, head_size = queries.shape
    tiles = seq_len // block_rows
    scale_value = head_size ** (-0.5)
    positions = jnp.arange(seq_len, dtype=jnp.int32)

    def query_block(carry, packed):
        key_acc, value_acc = carry
        query_tile, segment_tile, index_tile, total_tile, grad_tile = packed
        scores = masked_scores(
            query_tile, key_rows, segment_tile, index_tile, segments, scale_value
        )
        probs = jnp.exp(scores - total_tile[..., None])
        probs_low = probs.astype(jnp.bfloat16)
        prob_grad = jnp.einsum(
            "qhd,khd->hqk", grad_tile, value_rows, preferred_element_type=jnp.float32
        )
        score_grad = (
            probs * (prob_grad - jnp.sum(probs * prob_grad, axis=-1, keepdims=True))
        ).astype(jnp.bfloat16)
        query_grad = (
            jnp.einsum("hqk,khd->qhd", score_grad, key_rows, preferred_element_type=jnp.float32)
            * scale_value
        )
        key_acc = (
            key_acc
            + jnp.einsum("hqk,qhd->khd", score_grad, query_tile, preferred_element_type=jnp.float32)
            * scale_value
        )
        value_acc = value_acc + jnp.einsum(
            "hqk,qhd->khd", probs_low, grad_tile, preferred_element_type=jnp.float32
        )
        return ((key_acc, value_acc), query_grad)

    start_acc = (jnp.zeros(queries.shape, jnp.float32), jnp.zeros(queries.shape, jnp.float32))
    (key_grad, value_grad), query_grad = lax.scan(
        query_block,
        start_acc,
        (
            queries.reshape(tiles, block_rows, head_count, head_size),
            segments.reshape(tiles, block_rows),
            positions.reshape(tiles, block_rows),
            log_total,
            out_grad.reshape(tiles, block_rows, head_count, head_size),
        ),
    )
    return (query_grad.reshape(seq_len, head_count, head_size), key_grad, value_grad)


def gather_attention(qkv_weight, out_weight):
    return (
        lax.all_gather(qkv_weight, "fsdp", axis=0, tiled=True),
        lax.all_gather(out_weight, "fsdp", axis=0, tiled=True),
    )


def gather_feedforward(gate_up_weight, down_weight):
    return (
        lax.all_gather(gate_up_weight, "fsdp", axis=0, tiled=True),
        lax.all_gather(down_weight, "fsdp", axis=0, tiled=True),
    )


def per_device(
    block_in,
    out_cotangent,
    segment_ids,
    doc_positions,
    norm1_gain,
    qkv_weight,
    out_weight,
    norm2_gain,
    gate_up_weight,
    down_weight,
):
    micro_count = block_in.shape[0]
    fsdp_count = lax.axis_size("fsdp")
    segment_full, position_full = (
        lax.all_gather(segment_ids, "tp", axis=1, tiled=True),
        lax.all_gather(doc_positions, "tp", axis=1, tiled=True),
    )
    seq_len = segment_full.shape[1]
    block_rows = min(seq_len, 512)
    gain_one = norm1_gain.astype(jnp.float32)
    gain_two = norm2_gain.astype(jnp.float32)
    local_cols = qkv_weight.shape[2]
    local_units = gate_up_weight.shape[2]
    heads_local = local_cols // HD
    grad_qkv = jnp.zeros((D, 3, local_cols), jnp.float32)
    grad_out = jnp.zeros((out_weight.shape[0] * fsdp_count, D), jnp.float32)
    grad_gate_up = jnp.zeros((D, 2, local_units), jnp.float32)
    grad_down = jnp.zeros((down_weight.shape[0] * fsdp_count, D), jnp.float32)
    gain_one_acc = jnp.zeros((D,), jnp.float32)
    gain_two_acc = jnp.zeros((D,), jnp.float32)
    outputs = []
    input_grads = []
    for micro_index in range(micro_count):
        weights_fwd = (
            gather_attention(qkv_weight, out_weight),
            gather_feedforward(gate_up_weight, down_weight),
        )
        (qkv_full, out_full), (gate_up_full, down_full) = weights_fwd
        stream = block_in[micro_index].astype(jnp.float32)
        segment_row = segment_full[micro_index]
        cosine_part, sine_part = rope_tables(position_full[micro_index], HD)
        scale_one = rms_scale(stream)
        normed_one = (stream * scale_one * gain_one).astype(jnp.bfloat16)
        normed_one_full = lax.all_gather(normed_one, "tp", axis=0, tiled=True)
        projected = jnp.einsum(
            "sd,dtc->stc", normed_one_full, qkv_full, preferred_element_type=jnp.float32
        )
        queries = rotate(
            projected[:, 0].reshape(seq_len, heads_local, HD), cosine_part, sine_part
        ).astype(jnp.bfloat16)
        key_rows = rotate(
            projected[:, 1].reshape(seq_len, heads_local, HD), cosine_part, sine_part
        ).astype(jnp.bfloat16)
        value_rows = projected[:, 2].reshape(seq_len, heads_local, HD).astype(jnp.bfloat16)
        mixed, log_total = attention_forward(queries, key_rows, value_rows, segment_row, block_rows)
        attn_heads = mixed.astype(jnp.bfloat16)
        attn_term = jnp.dot(attn_heads, out_full, preferred_element_type=jnp.float32)
        attn_branch = lax.psum_scatter(attn_term, "tp", scatter_dimension=0, tiled=True)
        middle = stream + attn_branch
        scale_two = rms_scale(middle)
        normed_two = (middle * scale_two * gain_two).astype(jnp.bfloat16)
        normed_two_full = lax.all_gather(normed_two, "tp", axis=0, tiled=True)
        gate_up = jnp.einsum(
            "sd,dtf->stf", normed_two_full, gate_up_full, preferred_element_type=jnp.float32
        )
        gate_rows = gate_up[:, 0]
        up_rows = gate_up[:, 1]
        sigmoid_gate = jax.nn.sigmoid(gate_rows)
        silu_gate = gate_rows * sigmoid_gate
        activated = (silu_gate * up_rows).astype(jnp.bfloat16)
        mlp_term = jnp.dot(activated, down_full, preferred_element_type=jnp.float32)
        mlp_branch = lax.psum_scatter(
            mlp_term.astype(jnp.bfloat16), "tp", scatter_dimension=0, tiled=True
        ).astype(jnp.float32)
        outputs.append((middle + mlp_branch).astype(jnp.bfloat16))
        (qkv_back, out_back), (gate_up_back, down_back) = weights_fwd
        cotangent = out_cotangent[micro_index].astype(jnp.float32)
        cotangent_full = lax.all_gather(out_cotangent[micro_index], "tp", axis=0, tiled=True)
        grad_down = grad_down + jnp.einsum(
            "sf,sd->fd", activated, cotangent_full, preferred_element_type=jnp.float32
        )
        act_grad = jnp.einsum(
            "sd,fd->sf", cotangent_full, down_back, preferred_element_type=jnp.float32
        )
        gate_grad = act_grad * up_rows * sigmoid_gate * (1.0 + gate_rows * (1.0 - sigmoid_gate))
        up_grad = act_grad * silu_gate
        gate_up_grad = jnp.stack([gate_grad, up_grad], axis=1).astype(jnp.bfloat16)
        grad_gate_up = grad_gate_up + jnp.einsum(
            "sd,stf->dtf", normed_two_full, gate_up_grad, preferred_element_type=jnp.float32
        )
        normed_two_term = jnp.einsum(
            "stf,dtf->sd", gate_up_grad, gate_up_back, preferred_element_type=jnp.float32
        )
        normed_two_grad = lax.psum_scatter(normed_two_term, "tp", scatter_dimension=0, tiled=True)
        middle_back, gain_two_term = norm_back(middle, scale_two, gain_two, normed_two_grad)
        gain_two_acc = gain_two_acc + gain_two_term
        middle_grad = cotangent + middle_back
        attn_grad_full = lax.all_gather(middle_grad.astype(jnp.bfloat16), "tp", axis=0, tiled=True)
        grad_out = grad_out + jnp.einsum(
            "sc,sd->cd", attn_heads, attn_grad_full, preferred_element_type=jnp.float32
        )
        heads_grad = jnp.einsum(
            "sd,cd->sc", attn_grad_full, out_back, preferred_element_type=jnp.float32
        ).astype(jnp.bfloat16)
        query_grad, key_grad, value_grad = attention_backward(
            queries,
            key_rows,
            value_rows,
            segment_row,
            log_total,
            heads_grad.reshape(seq_len, heads_local, HD),
            block_rows,
        )
        projected_grad = jnp.stack(
            [
                unrotate(query_grad, cosine_part, sine_part).reshape(seq_len, local_cols),
                unrotate(key_grad, cosine_part, sine_part).reshape(seq_len, local_cols),
                value_grad.reshape(seq_len, local_cols),
            ],
            axis=1,
        ).astype(jnp.bfloat16)
        grad_qkv = grad_qkv + jnp.einsum(
            "sd,stc->dtc", normed_one_full, projected_grad, preferred_element_type=jnp.float32
        )
        normed_one_term = jnp.einsum(
            "stc,dtc->sd", projected_grad, qkv_back, preferred_element_type=jnp.float32
        )
        normed_one_grad = lax.psum_scatter(
            normed_one_term.astype(jnp.bfloat16), "tp", scatter_dimension=0, tiled=True
        ).astype(jnp.float32)
        stream_back, gain_one_term = norm_back(stream, scale_one, gain_one, normed_one_grad)
        gain_one_acc = gain_one_acc + gain_one_term
        input_grads.append(middle_grad + stream_back)
    owned_grads = (
        lax.psum_scatter(
            grad_qkv.astype(jnp.bfloat16), "fsdp", scatter_dimension=0, tiled=True
        ).astype(jnp.float32),
        lax.psum_scatter(
            grad_out.astype(jnp.bfloat16), "fsdp", scatter_dimension=0, tiled=True
        ).astype(jnp.float32),
        lax.psum_scatter(
            grad_gate_up.astype(jnp.bfloat16), "fsdp", scatter_dimension=0, tiled=True
        ).astype(jnp.float32),
        lax.psum_scatter(
            grad_down.astype(jnp.bfloat16), "fsdp", scatter_dimension=0, tiled=True
        ).astype(jnp.float32),
    )
    owned_gains = (
        lax.psum_scatter(gain_one_acc, ("fsdp", "tp"), scatter_dimension=0, tiled=True),
        lax.psum_scatter(gain_two_acc, ("fsdp", "tp"), scatter_dimension=0, tiled=True),
    )
    return (
        jnp.stack(outputs),
        jnp.stack(input_grads),
        owned_gains[0],
        owned_grads[0],
        owned_grads[1],
        owned_gains[1],
        owned_grads[2],
        owned_grads[3],
    )


def solution(mesh):
    in_specs = (
        P("fsdp", "tp", None),
        P("fsdp", "tp", None),
        P("fsdp", "tp"),
        P("fsdp", "tp"),
        P(),
        P("fsdp", None, "tp"),
        P(("tp", "fsdp"), None),
        P(),
        P("fsdp", None, "tp"),
        P(("tp", "fsdp"), None),
    )
    out_specs = (
        P("fsdp", "tp", None),
        P("fsdp", "tp", None),
        P(("fsdp", "tp")),
        P("fsdp", None, "tp"),
        P(("tp", "fsdp"), None),
        P(("fsdp", "tp")),
        P("fsdp", None, "tp"),
        P(("tp", "fsdp"), None),
    )
    return jax.shard_map(
        per_device, mesh=mesh, in_specs=in_specs, out_specs=out_specs, check_vma=False
    )
```

profile of v0, /device:TPU:0, one launch (start us, length us, event | category | flops | bytes accessed | tf_op | source)
XLA Modules:
  0.0 3195.4 jit_solution(16178268120911016994)
XLA Ops:
  53.0 79.6 %all-gather.15.cloned.1.call-done = bf16[1024,3072]{1,0:T(8,128)(2,1)} async-done(((bf16[256,3072]{1,0:T(8,128)(2,1)}), bf16[1024,3072]{1,0:T(8,128)(2,1)}) %all-gather.15.cloned.1.call-update) | async-done | bytes 6291472 | tf_op jit(solution)/shard_map/all_gather | solution.py:209
  132.6 82.2 %all-gather.17.cloned.1.call-done = bf16[3072,3,768]{0,2,1:T(8,128)(2,1)} async-done(((bf16[384,3,768]{0,2,1:T(8,128)(2,1)}), bf16[3072,3,768]{0,2,1:T(8,128)(2,1)}) %all-gather.17.cloned.1.call-update) | async-done | bytes 14155792 | tf_op jit(solution)/shard_map/all_gather | solution.py:153
  239.7 33.8 %while.54 = (s32[]{:T(128)}, bf16[2,512,8,96]{1,3,2,0:T(8,128)(2,1)}, f32[2,8,512]{2,1,0:T(8,128)S(1)}, s32[2,512]{1,0:T(2,128)S(1)}, s32[1,1024]{1,0:T(1,128)S(...) while((s32[]{:T(128)}, ...), condition=%wide.region_4.5_spmd, body=%wide.region_1.4_spmd.sunk | while | flops 1662513152 | bytes 70664376 | solution.py:91
  290.2 82.9 %all-gather.27.cloned.1.call-done = bf16[1024,3072]{1,0:T(8,128)(2,1)} async-done(((bf16[256,3072]{1,0:T(8,128)(2,1)}), bf16[1024,3072]{1,0:T(8,128)(2,1)}) %all-gather.27.cloned.1.call-update) | async-done | bytes 6291472 | tf_op jit(solution)/shard_map/all_gather | solution.py:209
  398.8 34.1 %while.55 = (s32[]{:T(128)}, bf16[2,512,8,96]{1,3,2,0:T(8,128)(2,1)}, f32[2,8,512]{2,1,0:T(8,128)S(1)}, s32[2,512]{1,0:T(2,128)S(1)}, s32[1,1024]{1,0:T(1,128)S(...) while((s32[]{:T(128)}, ...), condition=%wide.region_12.13_spmd, body=%wide.region_9.12_spmd.sunk | while | flops 1662513152 | bytes 70664376 | solution.py:91
  452.1 133.4 %reduce-scatter.13.cloned.1.call-done = f32[256,3072]{1,0:T(8,128)} async-done(((f32[1024,3072]{1,0:T(8,128)}), f32[256,3072]{1,0:T(8,128)}) %reduce-scatter.13.cloned.1.call-update) | async-done | bytes 3145744 | tf_op jit(solution)/shard_map/reduce_scatter | solution.py:223
  585.4 215.1 %reduce-scatter.17.cloned.1.call-done = f32[256,3072]{1,0:T(8,128)} async-done(((f32[1024,3072]{1,0:T(8,128)}), f32[256,3072]{1,0:T(8,128)}) %reduce-scatter.17.cloned.1.call-update) | async-done | bytes 3145744 | tf_op jit(solution)/shard_map/reduce_scatter | solution.py:223
  812.7 116.8 %all-gather.23.cloned.1.call-done = bf16[3072,2,2048]{2,0,1:T(8,128)(2,1)} async-done(((bf16[384,2,2048]{2,0,1:T(8,128)(2,1)}), bf16[3072,2,2048]{2,0,1:T(8,128)(2,1)}) %all-gather.23.cloned.1.call-update) | async-done | bytes 25165840 | tf_op jit(solution)/shard_map/all_gather | solution.py:160
  929.4 117.5 %all-gather.21.cloned.1.call-done = bf16[1024,3072]{1,0:T(8,128)(2,1)} async-done(((bf16[256,3072]{1,0:T(8,128)(2,1)}), bf16[1024,3072]{1,0:T(8,128)(2,1)}) %all-gather.21.cloned.1.call-update) | async-done | bytes 6291472 | tf_op jit(solution)/shard_map/all_gather | solution.py:227
  1047.0 33.4 %fusion.73 = f32[1024,2,2048]{2,0,1:T(8,128)} fusion(bf16[3072,2,2048]{2,0,1:T(8,128)(2,1)} %all-gather.23.cloned.1.call-done, bf16[1024,3072]{1,0:T(8,128)(2,1)} %all-gather.21.cloned.1.call-done), kind=kOutput, calls=%fused_computation.140 | convolution fusion | flops 25769803776 | bytes 48234496 | tf_op jit(solution)/shard_map/sd,dtf->stf/dot_general | solution.py:228
  1080.4 82.4 %all-gather.35.cloned.1.call-done = bf16[1,1024,3072]{2,1,0:T(8,128)(2,1)} async-done(((bf16[1,256,3072]{2,1,0:T(8,128)(2,1)}), bf16[1,1024,3072]{2,1,0:T(8,128)(2,1)}) %all-gather.35.cloned.1.call-update) | async-done | bytes 6291472 | tf_op jit(solution)/shard_map/all_gather | solution.py:243
  1162.7 72.1 %all-gather.25.cloned.1.call-done = bf16[2048,3072]{1,0:T(8,128)(2,1)} async-done(((bf16[256,3072]{1,0:T(8,128)(2,1)}), bf16[2048,3072]{1,0:T(8,128)(2,1)}) %all-gather.25.cloned.1.call-update) | async-done | bytes 12582928 | tf_op jit(solution)/shard_map/all_gather | solution.py:161
  1260.2 34.2 %convolution_bitcast_fusion.1 = f32[1024,3072]{1,0:T(8,128)} fusion(bf16[3072,2,2048]{2,0,1:T(8,128)(2,1)} %all-gather.23.cloned.1.call-done, bf16[1024,1,2048]{2,0,1:T(8,128)(2,1)} %get-tuple-element.541, bf16[1024,1,2048]{2,0,1:T(8,128)(2,1)} %get-tuple-element.540), kind=kOutput, calls=%fused_computation.123 | convolution fusion | flops 25773998080 | bytes 46137344 | tf_op jit(solution)/shard_map/stf,dtf->sd/dot_general | solution.py:256
  1295.0 211.4 %reduce-scatter.21.cloned.1.call-done = f32[256,3072]{1,0:T(8,128)} async-done(((f32[1024,3072]{1,0:T(8,128)}), f32[256,3072]{1,0:T(8,128)}) %reduce-scatter.21.cloned.1.call-update) | async-done | bytes 3145744 | tf_op jit(solution)/shard_map/reduce_scatter | solution.py:259
  1513.2 115.7 %all-gather.29.cloned.1.call-done = bf16[1024,3072]{1,0:T(8,128)(2,1)} async-done(((bf16[256,3072]{1,0:T(8,128)(2,1)}), bf16[1024,3072]{1,0:T(8,128)(2,1)}) %all-gather.29.cloned.1.call-update) | async-done | bytes 6291472 | tf_op jit(solution)/shard_map/all_gather | solution.py:227
  1628.9 33.4 %fusion.66 = f32[1024,2,2048]{2,0,1:T(8,128)} fusion(bf16[3072,2,2048]{2,0,1:T(8,128)(2,1)} %all-gather.23.cloned.1.call-done, bf16[1024,3072]{1,0:T(8,128)(2,1)} %all-gather.29.cloned.1.call-done), kind=kOutput, calls=%fused_computation.133 | convolution fusion | flops 25769803776 | bytes 48234496 | tf_op jit(solution)/shard_map/sd,dtf->stf/dot_general | solution.py:228
  1662.3 81.8 %all-gather.37.cloned.1.call-done = bf16[1,1024,3072]{2,1,0:T(8,128)(2,1)} async-done(((bf16[1,256,3072]{2,1,0:T(8,128)(2,1)}), bf16[1,1024,3072]{2,1,0:T(8,128)(2,1)}) %all-gather.37.cloned.1.call-update) | async-done | bytes 6291472 | tf_op jit(solution)/shard_map/all_gather | solution.py:243
  1769.4 33.9 %convolution_bitcast_fusion = f32[1024,3072]{1,0:T(8,128)} fusion(bf16[3072,2,2048]{2,0,1:T(8,128)(2,1)} %all-gather.23.cloned.1.call-done, bf16[1024,1,2048]{2,0,1:T(8,128)(2,1)} %get-tuple-element.543, bf16[1024,1,2048]{2,0,1:T(8,128)(2,1)} %get-tuple-element.542), kind=kOutput, calls=%fused_computation.122 | convolution fusion | flops 25773998080 | bytes 46137344 | tf_op jit(solution)/shard_map/stf,dtf->sd/dot_general | solution.py:256
  1840.8 172.8 %reduce-scatter.25.cloned.1.call-done = f32[256,3072]{1,0:T(8,128)} async-done(((f32[1024,3072]{1,0:T(8,128)}), f32[256,3072]{1,0:T(8,128)}) %reduce-scatter.25.cloned.1.call-update) | async-done | bytes 3145744 | tf_op jit(solution)/shard_map/reduce_scatter | solution.py:259
  2018.0 110.2 %reduce-scatter.15.cloned.1.call-done = bf16[256,3072]{1,0:T(8,128)(2,1)} async-done(((bf16[1024,3072]{1,0:T(8,128)(2,1)}), bf16[256,3072]{1,0:T(8,128)(2,1)}) %reduce-scatter.15.cloned.1.call-update) | async-done | bytes 1572880 | tf_op jit(solution)/shard_map/reduce_scatter | solution.py:237
  2128.2 114.0 %reduce-scatter.19.cloned.1.call-done = bf16[256,3072]{1,0:T(8,128)(2,1)} async-done(((bf16[1024,3072]{1,0:T(8,128)(2,1)}), bf16[256,3072]{1,0:T(8,128)(2,1)}) %reduce-scatter.19.cloned.1.call-update) | async-done | bytes 1572880 | tf_op jit(solution)/shard_map/reduce_scatter | solution.py:237
  2296.3 35.1 %fusion.71 = f32[3072,2,2048]{2,0,1:T(8,128)} fusion(bf16[1024,3072]{1,0:T(8,128)(2,1)} %all-gather.21.cloned.1.call-done, bf16[1024,1,2048]{2,0,1:T(8,128)(2,1)} %get-tuple-element.541, bf16[1024,1,2048]{2,0,1:T(8,128)(2,1)} %get-tuple-element.540), kind=kOutput, calls=%fused_computation.138 | convolution fusion | flops 25786580992 | bytes 65011712 | tf_op jit(solution)/shard_map/sd,stf->dtf/dot_general | solution.py:253
  2331.5 37.3 %add_convert_fusion = bf16[3072,2,2048]{2,0,1:T(8,128)(2,1)} fusion(f32[3072,2,2048]{2,0,1:T(8,128)} %fusion.71, bf16[1024,3072]{1,0:T(8,128)(2,1)} %all-gather.29.cloned.1.call-done, bf16[1024,1,2048]{2,0,1:T(8,128)(2,1)} %get-tuple-element.543, bf16[1024,1,2048]{2,0,1:T(8,128)(2,1)} %get-tuple-element.542), kind=kOutput, calls=%fused_computation.88 | convolution fusion | flops 25811746816 | bytes 90177536 | tf_op jit(solution)/shard_map/sd,stf->dtf/dot_general | solution.py:253
  2397.4 86.0 %all-gather.33.cloned.1.call-done = bf16[1024,3072]{1,0:T(8,128)(2,1)} async-done(((bf16[256,3072]{1,0:T(8,128)(2,1)}), bf16[1024,3072]{1,0:T(8,128)(2,1)}) %all-gather.33.cloned.1.call-update) | async-done | bytes 6291472 | tf_op jit(solution)/shard_map/all_gather | solution.py:263
  2496.8 193.2 %while.56 = (s32[]{:T(128)}, f32[1024,8,96]{0,2,1:T(8,128)S(1)}, f32[1024,8,96]{0,2,1:T(8,128)}, f32[2,512,8,96]{1,0,3,2:T(2,128)}, bf16[2,512,8,96]{1,3,2,0:T(8...) while((s32[]{:T(128)}, f32[1024,8,96]{0,2,1:T(8,128)S(1)}, ...), condition=%wide.region_20.21_spmd.clone, body=%wide.region_18.20_spmd.clone.sunk | while | flops 4070174720 | bytes 241271072 | solution.py:137
  2560.0 29.0 dynamic_update_slice.36
  2660.8 29.0 dynamic_update_slice.36
  2748.0 181.8 %while.57 = (s32[]{:T(128)}, f32[1024,8,96]{0,2,1:T(8,128)S(1)}, f32[1024,8,96]{0,2,1:T(8,128)}, f32[2,512,8,96]{1,0,3,2:T(2,128)}, bf16[2,512,8,96]{1,3,2,0:T(8...) while((s32[]{:T(128)}, f32[1024,8,96]{0,2,1:T(8,128)S(1)}, ...), condition=%wide.region_27.28_spmd.clone, body=%wide.region_25.27_spmd.clone.sunk | while | flops 4070174720 | bytes 234979584 | solution.py:137
  2900.5 28.9 dynamic_update_slice.37
  3032.2 46.8 %reduce-scatter.27.cloned.1.call-done = bf16[256,3072]{1,0:T(8,128)(2,1)} async-done(((bf16[1024,3072]{1,0:T(8,128)(2,1)}), bf16[256,3072]{1,0:T(8,128)(2,1)}) %reduce-scatter.27.cloned.1.call-update) | async-done | bytes 1572880 | tf_op jit(solution)/shard_map/reduce_scatter | solution.py:293
  3083.8 41.4 %all-reduce.2 = (f32[3072]{0:T(1024)S(1)}, f32[3072]{0:T(1024)S(1)}) all-reduce(f32[3072]{0:T(1024)S(1)} %add.229, f32[3072]{0:T(1024)S(1)} %add.232), channel_id=12, replica_groups=mesh['fsdp'=8,'tp'=4] {'fsdp','tp'}, use_global_device_ids=true, to_apply=%region_32.33.clone | all-reduce | flops 6144 | bytes 49152
  3134.8 50.0 %reduce-scatter.29.cloned.1.call-done = bf16[384,3,768]{2,0,1:T(8,128)(2,1)} async-done(((bf16[3072,3,768]{2,0,1:T(8,128)(2,1)}), bf16[384,3,768]{2,0,1:T(8,128)(2,1)}) %reduce-scatter.29.cloned.1.call-update) | async-done | bytes 1769488 | tf_op jit(solution)/shard_map/reduce_scatter | solution.py:300
  (411 shorter events, 871.6 us)
Async XLA Ops:
  7.2 125.4 %all-gather.15.cloned.1.call-start = ((), (), s32[]{:S(2)}) async-start(), calls=%async_computation.12 | async-start | bytes 7864320 | tf_op jit(solution)/shard_map/all_gather | solution.py:209
  14.2 200.6 %all-gather.17.cloned.1.call-start = ((), (), s32[]{:S(2)}) async-start(), calls=%async_computation.13 | async-start | bytes 15925248 | tf_op jit(solution)/shard_map/all_gather | solution.py:153
  18.1 261.2 %all-gather.19.cloned.1.call-start = ((), (), s32[]{:S(2)}) async-start(), calls=%async_computation.14 | async-start | bytes 5308416 | tf_op jit(solution)/shard_map/all_gather | solution.py:154
  18.9 354.2 %all-gather.27.cloned.1.call-start = ((), (), s32[]{:S(2)}) async-start(), calls=%async_computation.20 | async-start | bytes 7864320 | tf_op jit(solution)/shard_map/all_gather | solution.py:209
  19.5 566.0 %reduce-scatter.13.cloned.1.call-start = ((), (), s32[]{:S(2)}) async-start(), calls=%async_computation.15 | async-start | bytes 15728640 | tf_op jit(solution)/shard_map/reduce_scatter | solution.py:223
  289.5 511.0 %reduce-scatter.17.cloned.1.call-start = ((), (), s32[]{:S(2)}) async-start(), calls=%async_computation.21 | async-start | bytes 15728640 | tf_op jit(solution)/shard_map/reduce_scatter | solution.py:223
  447.0 482.5 %all-gather.23.cloned.1.call-start = ((), (), s32[]{:S(2)}) async-start(), calls=%async_computation.17 | async-start | bytes 28311552 | tf_op jit(solution)/shard_map/all_gather | solution.py:160
  452.0 348.6 %copy-start.14 = (bf16[2,256,3072]{2,1,0:T(8,128)(2,1)S(1)}, bf16[2,256,3072]{2,1,0:T(8,128)(2,1)}, u32[]{:S(2)}) copy-start(bf16[2,256,3072]{2,1,0:T(8,128)(2,1)} %param.18) | copy-start | bytes 9437188
  452.0 595.0 %all-gather.21.cloned.1.call-start = ((), (), s32[]{:S(2)}) async-start(), calls=%async_computation.16 | async-start | bytes 7864320 | tf_op jit(solution)/shard_map/all_gather | solution.py:227
  452.1 1054.3 %copy-start.56 = (f32[3072]{0:T(1024)}, f32[3072]{0:T(1024)S(1)}, u32[]{:S(2)}) copy-start(f32[3072]{0:T(1024)S(1)} %convert_element_type.185) | copy-start | bytes 36868
  806.5 699.9 %copy-start.66 = (f32[256]{0:T(256)}, f32[256]{0:T(256)S(1)}, u32[]{:S(2)}) copy-start(f32[256]{0:T(256)S(1)} %get-tuple-element.600) | copy-start | bytes 3076
  809.1 353.6 %all-gather.35.cloned.1.call-start = ((), (), s32[]{:S(2)}) async-start(), calls=%async_computation.34 | async-start | bytes 7864320 | tf_op jit(solution)/shard_map/all_gather | solution.py:243
  812.0 422.8 %all-gather.25.cloned.1.call-start = ((), (), s32[]{:S(2)}) async-start(), calls=%async_computation.18 | async-start | bytes 14155776 | tf_op jit(solution)/shard_map/all_gather | solution.py:161
  812.6 693.8 %reduce-scatter.21.cloned.1.call-start = ((), (), s32[]{:S(2)}) async-start(), calls=%async_computation.24 | async-start | bytes 15728640 | tf_op jit(solution)/shard_map/reduce_scatter | solution.py:259
  1294.4 334.5 %all-gather.29.cloned.1.call-start = ((), (), s32[]{:S(2)}) async-start(), calls=%async_computation.22 | async-start | bytes 7864320 | tf_op jit(solution)/shard_map/all_gather | solution.py:227
  1295.0 217.3 %copy-start.68 = (f32[256]{0:T(256)}, f32[256]{0:T(256)S(1)}, u32[]{:S(2)}) copy-start(f32[256]{0:T(256)S(1)} %get-tuple-element.602) | copy-start | bytes 3076
  1512.4 231.7 %all-gather.37.cloned.1.call-start = ((), (), s32[]{:S(2)}) async-start(), calls=%async_computation.35 | async-start | bytes 7864320 | tf_op jit(solution)/shard_map/all_gather | solution.py:243
  1513.1 500.5 %reduce-scatter.25.cloned.1.call-start = ((), (), s32[]{:S(2)}) async-start(), calls=%async_computation.27 | async-start | bytes 15728640 | tf_op jit(solution)/shard_map/reduce_scatter | solution.py:259
  1803.4 324.8 %reduce-scatter.15.cloned.1.call-start = ((), (), s32[]{:S(2)}) async-start(), calls=%async_computation.19 | async-start | bytes 7864320 | tf_op jit(solution)/shard_map/reduce_scatter | solution.py:237
  1821.8 420.4 %reduce-scatter.19.cloned.1.call-start = ((), (), s32[]{:S(2)}) async-start(), calls=%async_computation.23 | async-start | bytes 7864320 | tf_op jit(solution)/shard_map/reduce_scatter | solution.py:237
  1840.2 528.9 %all-gather.31.cloned.1.call-start = ((), (), s32[]{:S(2)}) async-start(), calls=%async_computation.25 | async-start | bytes 7864320 | tf_op jit(solution)/shard_map/all_gather | solution.py:263
  1840.8 401.4 %copy-start.18 = (f32[256,3072]{1,0:T(8,128)S(1)}, f32[256,3072]{1,0:T(8,128)}, u32[]{:S(2)}) copy-start(f32[256,3072]{1,0:T(8,128)} %copy-done.16) | copy-start | bytes 9437188
  1840.8 401.4 %copy-start.67 = (f32[256]{0:T(256)S(1)}, f32[256]{0:T(256)}, u32[]{:S(2)}) copy-start(f32[256]{0:T(256)} %copy-done.66) | copy-start | bytes 3076
  1840.8 401.4 %copy-start.76 = (f32[256]{0:T(256)S(1)}, f32[256]{0:T(256)}, u32[]{:S(2)}) copy-start(f32[256]{0:T(256)} %get-tuple-element.599) | copy-start | bytes 3076
  1840.8 401.4 %copy-start.77 = (f32[256]{0:T(256)S(1)}, f32[256]{0:T(256)}, u32[]{:S(2)}) copy-start(f32[256]{0:T(256)} %get-tuple-element.601) | copy-start | bytes 3076
  2252.3 231.1 %all-gather.33.cloned.1.call-start = ((), (), s32[]{:S(2)}) async-start(), calls=%async_computation.28 | async-start | bytes 7864320 | tf_op jit(solution)/shard_map/all_gather | solution.py:263
  2252.9 763.4 %reduce-scatter.35.cloned.1.call-start = ((), (), s32[]{:S(2)}) async-start(), calls=%async_computation.33 | async-start | bytes 14155776 | tf_op jit(solution)/shard_map/reduce_scatter | solution.py:309
  2296.1 725.8 %reduce-scatter.33.cloned.1.call-start = ((), (), s32[]{:S(2)}) async-start(), calls=%async_computation.32 | async-start | bytes 28311552 | tf_op jit(solution)/shard_map/reduce_scatter | solution.py:306
  2368.8 661.2 %reduce-scatter.31.cloned.1.call-start = ((), (), s32[]{:S(2)}) async-start(), calls=%async_computation.31 | async-start | bytes 5308416 | tf_op jit(solution)/shard_map/reduce_scatter | solution.py:303
  2493.8 538.4 %reduce-scatter.23.cloned.1.call-start = ((), (), s32[]{:S(2)}) async-start(), calls=%async_computation.26 | async-start | bytes 7864320 | tf_op jit(solution)/shard_map/reduce_scatter | solution.py:293
  2745.3 333.8 %reduce-scatter.27.cloned.1.call-start = ((), (), s32[]{:S(2)}) async-start(), calls=%async_computation.29 | async-start | bytes 7864320 | tf_op jit(solution)/shard_map/reduce_scatter | solution.py:293
  2968.7 216.1 %reduce-scatter.29.cloned.1.call-start = ((), (), s32[]{:S(2)}) async-start(), calls=%async_computation.30 | async-start | bytes 15925248 | tf_op jit(solution)/shard_map/reduce_scatter | solution.py:300
  (86 other events, 1729.6 us)
Sparse Core Ops, SparseCore 0:
  14.3 118.2 all-gather.14
  135.0 79.7 all-gather.16
  216.7 38.9 all-gather.18
  257.7 115.4 all-gather.26
  375.3 210.0 reduce-scatter.12
  587.6 212.8 reduce-scatter.16
  803.0 126.3 all-gather.22
  931.6 115.3 all-gather.20
  1049.1 113.5 all-gather.34
  1164.5 70.3 all-gather.24
  1294.5 211.8 reduce-scatter.20
  1512.5 116.3 all-gather.28
  1630.5 113.5 all-gather.36
  1803.5 210.0 reduce-scatter.24
  2016.3 111.7 reduce-scatter.14
  2130.9 111.2 reduce-scatter.18
  2252.5 115.8 all-gather.30
  2369.8 113.5 all-gather.32
  2486.9 90.6 reduce-scatter.34
  2581.0 156.8 reduce-scatter.32
  2741.4 53.8 reduce-scatter.30
  2798.3 110.7 reduce-scatter.22
  2968.8 110.1 reduce-scatter.26
  3082.9 101.8 reduce-scatter.28
where the time goes:
time: 3210 us; the launch traced here: 3200 us
  waiting for transfers between devices  1970 us (61%)
  matrix products  733 us (23%)
  local copies, waits for them, and re-layouts  233 us (7%)
  other arithmetic  165 us (5%)
  blocking collectives  71.3 us (2%)
    reduce_scatter x2, waiting for transfers between devices, per_device(): lax.psum_scatter(normed_two_term, 'tp', scatter_dimension=0, tiled=True)  384 us
    reduce_scatter x2, waiting for transfers between devices, per_device(): lax.psum_scatter(attn_term, 'tp', scatter_dimension=0, tiled=True)  348 us
    all_gather x2, waiting for transfers between devices, per_device(): normed_two_full = lax.all_gather(normed_two, 'tp', axis=0, tiled=True)  233 us
    reduce_scatter x2, waiting for transfers between devices, per_device(): lax.psum_scatter(mlp_term.astype(jnp.bfloat16), 'tp', scatter_dimension=0...  224 us
    all_gather x2, waiting for transfers between devices, per_device(): lax.all_gather(out_cotangent[micro_index], 'tp', axis=0, tiled=True)  164 us
    all_gather x2, waiting for transfers between devices, per_device(): normed_one_full = lax.all_gather(normed_one, 'tp', axis=0, tiled=True)  163 us
    dynamic_update_slice x8, local copies, waits for them, and re-layouts, attention_forward(): lax.map(query_block, (queries.reshape(tiles, block_rows, head_count, head...  127 us
    all_gather x1, waiting for transfers between devices, gather_feedforward(): lax.all_gather(gate_up_weight, 'fsdp', axis=0, tiled=True)  117 us
  transfers between devices with their start and end apart: 24, of which 18 were waited for; matrix products, arithmetic and copies ran while one was open for 30% of the time, Pallas kernels for 0%

commit v1 on v0

--- a/solution.py
+++ b/solution.py
@@ -8,6 +8,18 @@
 rms_epsilon = 1e-05
 rope_theta = 10000.0
 masked_score = -1e30
+
+
+def collect(value, axis, dim):
+    ways, here, lap = (lax.axis_size(axis), lax.axis_index(axis), value.shape[dim])
+    line, have = (value, 1)
+    while have < ways:
+        line = jnp.concatenate(
+            [line, lax.ppermute(line, axis, [(d, (d - have) % ways) for d in range(ways)])],
+            axis=dim,
+        )
+        have = 2 * have
+    return jnp.roll(line, here * lap, axis=dim)
 
 
 def rope_tables(positions, head_size):
@@ -260,7 +272,7 @@
         middle_back, gain_two_term = norm_back(middle, scale_two, gain_two, normed_two_grad)
         gain_two_acc = gain_two_acc + gain_two_term
         middle_grad = cotangent + middle_back
-        attn_grad_full = lax.all_gather(middle_grad.astype(jnp.bfloat16), "tp", axis=0, tiled=True)
+        attn_grad_full = collect(middle_grad.astype(jnp.bfloat16), "tp", 0)
         grad_out = grad_out + jnp.einsum(
             "sc,sd->cd", attn_heads, attn_grad_full, preferred_element_type=jnp.float32
         )

time: 3210 us -> 3420 us (1.065)
  waiting for transfers between devices: 1970 us -> 2140 us
  other arithmetic: 165 us -> 205 us
    ppermute x0 -> x4, waiting for transfers between devices: none -> 292 us  [collect(): lax.ppermute(line, axis, [(d, (d - have) % ways) for d in range(ways)])]
    all_gather x2 -> x0, waiting for transfers between devices: 86 us -> none  [per_device(): lax.all_gather(middle_grad.astype(jnp.bfloat16), 'tp', axis=0, tiled=True)]
    reduce_scatter x2, waiting for transfers between devices: 384 us -> 341 us  [per_device(): lax.psum_scatter(normed_two_term, 'tp', scatter_dimension=0, tiled=True)]
    concatenate x0 -> x4, other arithmetic: none -> 40.2 us  [the longest x2 36.9 us: collect(): return jnp.roll(line, here * lap, axis=dim)]
  transfers between devices with their start and end apart: 24 -> 26, of which waited for: 18 -> 20; matrix products, arithmetic and copies ran while one was open for 30% -> 29% of each run, Pallas kernels for 0% -> 0%
where the time goes in v1:
time: 3420 us; the launch traced here: 3410 us
  waiting for transfers between devices  2140 us (63%)
  matrix products  726 us (21%)
  local copies, waits for them, and re-layouts  234 us (7%)
  other arithmetic  205 us (6%)
  blocking collectives  71.3 us (2%)
    reduce_scatter x2, waiting for transfers between devices, per_device(): lax.psum_scatter(attn_term, 'tp', scatter_dimension=0, tiled=True)  349 us
    reduce_scatter x2, waiting for transfers between devices, per_device(): lax.psum_scatter(normed_two_term, 'tp', scatter_dimension=0, tiled=True)  341 us
    ppermute x4, waiting for transfers between devices, collect(): lax.ppermute(line, axis, [(d, (d - have) % ways) for d in range(ways)])  292 us
    all_gather x2, waiting for transfers between devices, per_device(): normed_two_full = lax.all_gather(normed_two, 'tp', axis=0, tiled=True)  233 us
    reduce_scatter x2, waiting for transfers between devices, per_device(): lax.psum_scatter(mlp_term.astype(jnp.bfloat16), 'tp', scatter_dimension=0...  224 us
    all_gather x2, waiting for transfers between devices, per_device(): lax.all_gather(out_cotangent[micro_index], 'tp', axis=0, tiled=True)  164 us
    all_gather x2, waiting for transfers between devices, per_device(): normed_one_full = lax.all_gather(normed_one, 'tp', axis=0, tiled=True)  162 us
    dynamic_update_slice x8, local copies, waits for them, and re-layouts, attention_forward(): lax.map(query_block, (queries.reshape(tiles, block_rows, head_count, head...  127 us
  transfers between devices with their start and end apart: 26, of which 20 were waited for; matrix products, arithmetic and copies ran while one was open for 29% of the time, Pallas kernels for 0%

profile of v1, /device:TPU:0, one launch (start us, length us, event | category | flops | bytes accessed | tf_op | source)
XLA Modules:
  0.0 3405.0 jit_solution(17081230155773689960)
XLA Ops:
  52.9 79.6 %all-gather.13.cloned.1.call-done = bf16[1024,3072]{1,0:T(8,128)(2,1)} async-done(((bf16[256,3072]{1,0:T(8,128)(2,1)}), bf16[1024,3072]{1,0:T(8,128)(2,1)}) %all-gather.13.cloned.1.call-update) | async-done | bytes 6291472 | tf_op jit(solution)/shard_map/all_gather | solution.py:221
  132.5 82.2 %all-gather.15.cloned.1.call-done = bf16[3072,3,768]{0,2,1:T(8,128)(2,1)} async-done(((bf16[384,3,768]{0,2,1:T(8,128)(2,1)}), bf16[3072,3,768]{0,2,1:T(8,128)(2,1)}) %all-gather.15.cloned.1.call-update) | async-done | bytes 14155792 | tf_op jit(solution)/shard_map/all_gather | solution.py:165
  239.6 34.1 %while.54 = (s32[]{:T(128)}, bf16[2,512,8,96]{1,3,2,0:T(8,128)(2,1)}, f32[2,8,512]{2,1,0:T(8,128)S(1)}, s32[2,512]{1,0:T(2,128)S(1)}, s32[1,1024]{1,0:T(1,128)S(...) while((s32[]{:T(128)}, ...), condition=%wide.region_4.5_spmd, body=%wide.region_1.4_spmd.sunk | while | flops 1662513152 | bytes 70664376 | solution.py:103
  290.4 82.6 %all-gather.25.cloned.1.call-done = bf16[1024,3072]{1,0:T(8,128)(2,1)} async-done(((bf16[256,3072]{1,0:T(8,128)(2,1)}), bf16[1024,3072]{1,0:T(8,128)(2,1)}) %all-gather.25.cloned.1.call-update) | async-done | bytes 6291472 | tf_op jit(solution)/shard_map/all_gather | solution.py:221
  398.6 33.9 while.55
  451.6 133.8 %reduce-scatter.13.cloned.1.call-done = f32[256,3072]{1,0:T(8,128)} async-done(((f32[1024,3072]{1,0:T(8,128)}), f32[256,3072]{1,0:T(8,128)}) %reduce-scatter.13.cloned.1.call-update) | async-done | bytes 3145744 | tf_op jit(solution)/shard_map/reduce_scatter | solution.py:235
  585.3 215.1 %reduce-scatter.17.cloned.1.call-done = f32[256,3072]{1,0:T(8,128)} async-done(((f32[1024,3072]{1,0:T(8,128)}), f32[256,3072]{1,0:T(8,128)}) %reduce-scatter.17.cloned.1.call-update) | async-done | bytes 3145744 | tf_op jit(solution)/shard_map/reduce_scatter | solution.py:235
  812.6 116.8 %all-gather.21.cloned.1.call-done = bf16[3072,2,2048]{2,0,1:T(8,128)(2,1)} async-done(((bf16[384,2,2048]{2,0,1:T(8,128)(2,1)}), bf16[3072,2,2048]{2,0,1:T(8,128)(2,1)}) %all-gather.21.cloned.1.call-update) | async-done | bytes 25165840 | tf_op jit(solution)/shard_map/all_gather | solution.py:172
  929.4 117.5 %all-gather.19.cloned.1.call-done = bf16[1024,3072]{1,0:T(8,128)(2,1)} async-done(((bf16[256,3072]{1,0:T(8,128)(2,1)}), bf16[1024,3072]{1,0:T(8,128)(2,1)}) %all-gather.19.cloned.1.call-update) | async-done | bytes 6291472 | tf_op jit(solution)/shard_map/all_gather | solution.py:239
  1046.9 33.3 fusion.83
  1080.2 82.5 %all-gather.29.cloned.1.call-done = bf16[1,1024,3072]{2,1,0:T(8,128)(2,1)} async-done(((bf16[1,256,3072]{2,1,0:T(8,128)(2,1)}), bf16[1,1024,3072]{2,1,0:T(8,128)(2,1)}) %all-gather.29.cloned.1.call-update) | async-done | bytes 6291472 | tf_op jit(solution)/shard_map/all_gather | solution.py:255
  1162.7 72.1 %all-gather.23.cloned.1.call-done = bf16[2048,3072]{1,0:T(8,128)(2,1)} async-done(((bf16[256,3072]{1,0:T(8,128)(2,1)}), bf16[2048,3072]{1,0:T(8,128)(2,1)}) %all-gather.23.cloned.1.call-update) | async-done | bytes 12582928 | tf_op jit(solution)/shard_map/all_gather | solution.py:173
  1260.1 33.9 convolution_bitcast_fusion.1
  1294.6 211.4 %reduce-scatter.21.cloned.1.call-done = f32[256,3072]{1,0:T(8,128)} async-done(((f32[1024,3072]{1,0:T(8,128)}), f32[256,3072]{1,0:T(8,128)}) %reduce-scatter.21.cloned.1.call-update) | async-done | bytes 3145744 | tf_op jit(solution)/shard_map/reduce_scatter | solution.py:271
  1512.8 115.8 %all-gather.27.cloned.1.call-done = bf16[1024,3072]{1,0:T(8,128)(2,1)} async-done(((bf16[256,3072]{1,0:T(8,128)(2,1)}), bf16[1024,3072]{1,0:T(8,128)(2,1)}) %all-gather.27.cloned.1.call-update) | async-done | bytes 6291472 | tf_op jit(solution)/shard_map/all_gather | solution.py:239
  1628.5 33.3 fusion.76
  1661.8 81.9 %all-gather.31.cloned.1.call-done = bf16[1,1024,3072]{2,1,0:T(8,128)(2,1)} async-done(((bf16[1,256,3072]{2,1,0:T(8,128)(2,1)}), bf16[1,1024,3072]{2,1,0:T(8,128)(2,1)}) %all-gather.31.cloned.1.call-update) | async-done | bytes 6291472 | tf_op jit(solution)/shard_map/all_gather | solution.py:255
  1769.0 34.1 %convolution_bitcast_fusion = f32[1024,3072]{1,0:T(8,128)} fusion(bf16[3072,2,2048]{2,0,1:T(8,128)(2,1)} %all-gather.21.cloned.1.call-done, bf16[1024,1,2048]{2,0,1:T(8,128)(2,1)} %get-tuple-element.544, bf16[1024,1,2048]{2,0,1:T(8,128)(2,1)} %get-tuple-element.543), kind=kOutput, calls=%fused_computation.134 | convolution fusion | flops 25773998080 | bytes 46137344 | tf_op jit(solution)/shard_map/stf,dtf->sd/dot_general | solution.py:268
  1883.8 129.5 %reduce-scatter.25.cloned.1.call-done = f32[256,3072]{1,0:T(8,128)} async-done(((f32[1024,3072]{1,0:T(8,128)}), f32[256,3072]{1,0:T(8,128)}) %reduce-scatter.25.cloned.1.call-update) | async-done | bytes 3145744 | tf_op jit(solution)/shard_map/reduce_scatter | solution.py:271
  2017.7 110.2 %reduce-scatter.15.cloned.1.call-done = bf16[256,3072]{1,0:T(8,128)(2,1)} async-done(((bf16[1024,3072]{1,0:T(8,128)(2,1)}), bf16[256,3072]{1,0:T(8,128)(2,1)}) %reduce-scatter.15.cloned.1.call-update) | async-done | bytes 1572880 | tf_op jit(solution)/shard_map/reduce_scatter | solution.py:249
  2127.9 114.0 %reduce-scatter.19.cloned.1.call-done = bf16[256,3072]{1,0:T(8,128)(2,1)} async-done(((bf16[1024,3072]{1,0:T(8,128)(2,1)}), bf16[256,3072]{1,0:T(8,128)(2,1)}) %reduce-scatter.19.cloned.1.call-update) | async-done | bytes 1572880 | tf_op jit(solution)/shard_map/reduce_scatter | solution.py:249
  2256.8 33.1 collective-permute-done
  2328.3 35.2 %fusion.81 = f32[3072,2,2048]{2,0,1:T(8,128)} fusion(bf16[1024,3072]{1,0:T(8,128)(2,1)} %all-gather.19.cloned.1.call-done, bf16[1024,1,2048]{2,0,1:T(8,128)(2,1)} %get-tuple-element.542, bf16[1024,1,2048]{2,0,1:T(8,128)(2,1)} %get-tuple-element.541), kind=kOutput, calls=%fused_computation.160 | convolution fusion | flops 25786580992 | bytes 65011712 | tf_op jit(solution)/shard_map/sd,stf->dtf/dot_general | solution.py:265
  2363.5 229.8 %collective-permute-done.3 = bf16[512,3072]{1,0:T(8,128)(2,1)S(1)} collective-permute-done((bf16[512,3072]{1,0:T(8,128)(2,1)S(1)}, bf16[512,3072]{1,0:T(8,128)(2,1)S(1)}, u32[]{:S(2)}, u32[]{:S(2)}) %collective-permute-start.3) | collective-permute-done | bytes 3145760 | tf_op jit(solution)/shard_map/ppermute | solution.py:18
  2647.3 38.3 %add_convert_fusion = bf16[3072,2,2048]{2,0,1:T(8,128)(2,1)} fusion(f32[3072,2,2048]{2,0,1:T(8,128)} %fusion.81, bf16[1024,3072]{1,0:T(8,128)(2,1)} %all-gather.27.cloned.1.call-done, bf16[1024,1,2048]{2,0,1:T(8,128)(2,1)} %get-tuple-element.544, bf16[1024,1,2048]{2,0,1:T(8,128)(2,1)} %get-tuple-element.543), kind=kOutput, calls=%fused_computation.88 | convolution fusion | flops 25811746816 | bytes 90177536 | tf_op jit(solution)/shard_map/sd,stf->dtf/dot_general | solution.py:265
  2706.9 192.7 %while.56 = (s32[]{:T(128)}, f32[1024,8,96]{0,2,1:T(8,128)S(1)}, f32[1024,8,96]{0,2,1:T(8,128)}, f32[2,512,8,96]{1,0,3,2:T(2,128)}, bf16[2,512,8,96]{1,3,2,0:T(8...) while((s32[]{:T(128)}, f32[1024,8,96]{0,2,1:T(8,128)S(1)}, ...), condition=%wide.region_20.22_spmd.clone, body=%wide.region_18.21_spmd.clone.sunk | while | flops 4070174720 | bytes 241271072 | solution.py:149
  2778.3 29.0 dynamic_update_slice.36
  2957.4 180.5 %while.57 = (s32[]{:T(128)}, f32[1024,8,96]{0,2,1:T(8,128)S(1)}, f32[1024,8,96]{0,2,1:T(8,128)}, f32[2,512,8,96]{1,0,3,2:T(2,128)}, bf16[2,512,8,96]{1,3,2,0:T(8...) while((s32[]{:T(128)}, f32[1024,8,96]{0,2,1:T(8,128)S(1)}, ...), condition=%wide.region_27.29_spmd.clone, body=%wide.region_25.28_spmd.clone.sunk | while | flops 4070174720 | bytes 234979584 | solution.py:149
  3018.4 28.9 dynamic_update_slice.37
  3240.2 48.2 %reduce-scatter.27.cloned.1.call-done = bf16[256,3072]{1,0:T(8,128)(2,1)} async-done(((bf16[1024,3072]{1,0:T(8,128)(2,1)}), bf16[256,3072]{1,0:T(8,128)(2,1)}) %reduce-scatter.27.cloned.1.call-update) | async-done | bytes 1572880 | tf_op jit(solution)/shard_map/reduce_scatter | solution.py:305
  3293.2 41.4 %all-reduce.2 = (f32[3072]{0:T(1024)S(1)}, f32[3072]{0:T(1024)S(1)}) all-reduce(f32[3072]{0:T(1024)S(1)} %add.237, f32[3072]{0:T(1024)S(1)} %add.240), channel_id=12, replica_groups=mesh['fsdp'=8,'tp'=4] {'fsdp','tp'}, use_global_device_ids=true, to_apply=%region_32.34.clone | all-reduce | flops 6144 | bytes 49152
  3344.2 50.2 %reduce-scatter.29.cloned.1.call-done = bf16[384,3,768]{2,0,1:T(8,128)(2,1)} async-done(((bf16[3072,3,768]{2,0,1:T(8,128)(2,1)}), bf16[384,3,768]{2,0,1:T(8,128)(2,1)}) %reduce-scatter.29.cloned.1.call-update) | async-done | bytes 1769488 | tf_op jit(solution)/shard_map/reduce_scatter | solution.py:312
  (427 shorter events, 973.6 us)
Async XLA Ops:
  7.2 125.4 %all-gather.13.cloned.1.call-start = ((), (), s32[]{:S(2)}) async-start(), calls=%async_computation.12 | async-start | bytes 7864320 | tf_op jit(solution)/shard_map/all_gather | solution.py:221
  14.2 200.6 %all-gather.15.cloned.1.call-start = ((), (), s32[]{:S(2)}) async-start(), calls=%async_computation.13 | async-start | bytes 15925248 | tf_op jit(solution)/shard_map/all_gather | solution.py:165
  18.1 261.5 %all-gather.17.cloned.1.call-start = ((), (), s32[]{:S(2)}) async-start(), calls=%async_computation.14 | async-start | bytes 5308416 | tf_op jit(solution)/shard_map/all_gather | solution.py:166
  18.8 354.2 %all-gather.25.cloned.1.call-start = ((), (), s32[]{:S(2)}) async-start(), calls=%async_computation.20 | async-start | bytes 7864320 | tf_op jit(solution)/shard_map/all_gather | solution.py:221
  19.4 565.9 %reduce-scatter.13.cloned.1.call-start = ((), (), s32[]{:S(2)}) async-start(), calls=%async_computation.15 | async-start | bytes 15728640 | tf_op jit(solution)/shard_map/reduce_scatter | solution.py:235
  289.7 510.8 %reduce-scatter.17.cloned.1.call-start = ((), (), s32[]{:S(2)}) async-start(), calls=%async_computation.21 | async-start | bytes 15728640 | tf_op jit(solution)/shard_map/reduce_scatter | solution.py:235
  446.5 482.9 %all-gather.21.cloned.1.call-start = ((), (), s32[]{:S(2)}) async-start(), calls=%async_computation.17 | async-start | bytes 28311552 | tf_op jit(solution)/shard_map/all_gather | solution.py:172
  451.5 595.4 %all-gather.19.cloned.1.call-start = ((), (), s32[]{:S(2)}) async-start(), calls=%async_computation.16 | async-start | bytes 7864320 | tf_op jit(solution)/shard_map/all_gather | solution.py:239
  451.6 1054.4 %copy-start.60 = (f32[3072]{0:T(1024)}, f32[3072]{0:T(1024)S(1)}, u32[]{:S(2)}) copy-start(f32[3072]{0:T(1024)S(1)} %convert_element_type.185) | copy-start | bytes 36868
  806.4 699.6 %copy-start.70 = (f32[256]{0:T(256)}, f32[256]{0:T(256)S(1)}, u32[]{:S(2)}) copy-start(f32[256]{0:T(256)S(1)} %get-tuple-element.601) | copy-start | bytes 3076
  809.1 353.6 %all-gather.29.cloned.1.call-start = ((), (), s32[]{:S(2)}) async-start(), calls=%async_computation.32 | async-start | bytes 7864320 | tf_op jit(solution)/shard_map/all_gather | solution.py:255
  811.9 422.9 %all-gather.23.cloned.1.call-start = ((), (), s32[]{:S(2)}) async-start(), calls=%async_computation.18 | async-start | bytes 14155776 | tf_op jit(solution)/shard_map/all_gather | solution.py:173
  812.5 693.4 %reduce-scatter.21.cloned.1.call-start = ((), (), s32[]{:S(2)}) async-start(), calls=%async_computation.24 | async-start | bytes 15728640 | tf_op jit(solution)/shard_map/reduce_scatter | solution.py:271
  1294.0 334.6 %all-gather.27.cloned.1.call-start = ((), (), s32[]{:S(2)}) async-start(), calls=%async_computation.22 | async-start | bytes 7864320 | tf_op jit(solution)/shard_map/all_gather | solution.py:239
  1512.0 231.7 %all-gather.31.cloned.1.call-start = ((), (), s32[]{:S(2)}) async-start(), calls=%async_computation.33 | async-start | bytes 7864320 | tf_op jit(solution)/shard_map/all_gather | solution.py:255
  1512.7 500.6 %reduce-scatter.25.cloned.1.call-start = ((), (), s32[]{:S(2)}) async-start(), calls=%async_computation.26 | async-start | bytes 15728640 | tf_op jit(solution)/shard_map/reduce_scatter | solution.py:271
  1803.1 324.8 %reduce-scatter.15.cloned.1.call-start = ((), (), s32[]{:S(2)}) async-start(), calls=%async_computation.19 | async-start | bytes 7864320 | tf_op jit(solution)/shard_map/reduce_scatter | solution.py:249
  1821.5 420.4 %reduce-scatter.19.cloned.1.call-start = ((), (), s32[]{:S(2)}) async-start(), calls=%async_computation.23 | async-start | bytes 7864320 | tf_op jit(solution)/shard_map/reduce_scatter | solution.py:249
  1839.9 1384.5 %reduce-scatter.35.cloned.1.call-start = ((), (), s32[]{:S(2)}) async-start(), calls=%async_computation.31 | async-start | bytes 14155776 | tf_op jit(solution)/shard_map/reduce_scatter | solution.py:321
  1883.2 1346.7 %reduce-scatter.31.cloned.1.call-start = ((), (), s32[]{:S(2)}) async-start(), calls=%async_computation.29 | async-start | bytes 5308416 | tf_op jit(solution)/shard_map/reduce_scatter | solution.py:315
  1883.8 358.1 %copy-start.18 = (f32[256,3072]{1,0:T(8,128)S(1)}, f32[256,3072]{1,0:T(8,128)}, u32[]{:S(2)}) copy-start(f32[256,3072]{1,0:T(8,128)} %copy-done.16) | copy-start | bytes 9437188
  1883.8 358.1 %copy-start.71 = (f32[256]{0:T(256)S(1)}, f32[256]{0:T(256)}, u32[]{:S(2)}) copy-start(f32[256]{0:T(256)} %copy-done.70) | copy-start | bytes 3076
  1883.8 358.1 %copy-start.80 = (f32[256]{0:T(256)S(1)}, f32[256]{0:T(256)}, u32[]{:S(2)}) copy-start(f32[256]{0:T(256)} %get-tuple-element.600) | copy-start | bytes 3076
  1883.8 358.1 %copy-start.81 = (f32[256]{0:T(256)S(1)}, f32[256]{0:T(256)}, u32[]{:S(2)}) copy-start(f32[256]{0:T(256)} %get-tuple-element.602) | copy-start | bytes 3076
  2252.4 37.6 %collective-permute-start = (bf16[256,3072]{1,0:T(8,128)(2,1)}, bf16[256,3072]{1,0:T(8,128)(2,1)S(1)}, u32[]{:S(2)}, u32[]{:S(2)}) collective-permute-start(bf16[256,3072]{1,0:T(8,128)(2,1)} %get-tuple-element.517), channel_id=1, source_target_pairs={{0,3},{1,0},{2,1},{3,2},{4,7},{5,4},{6,5},{7,6},{8,11},{9,8},{10,9... | collective-permute-start | bytes 4718600 | tf_op jit(solution)/shard_map/ppermute | solution.py:18
  2254.7 68.8 %collective-permute-start.2 = (bf16[256,3072]{1,0:T(8,128)(2,1)}, bf16[256,3072]{1,0:T(8,128)(2,1)S(1)}, u32[]{:S(2)}, u32[]{:S(2)}) collective-permute-start(bf16[256,3072]{1,0:T(8,128)(2,1)} %get-tuple-element.569), channel_id=1, source_target_pairs={{0,3},{1,0},{2,1},{3,2},{4,7},{5,4},{6,5},{7,6},{8,11},{9,8},{10,9... | collective-permute-start | bytes 4718600 | tf_op jit(solution)/shard_map/ppermute | solution.py:18
  2291.6 327.6 %collective-permute-start.1 = (bf16[512,3072]{1,0:T(8,128)(2,1)S(1)}, bf16[512,3072]{1,0:T(8,128)(2,1)S(1)}, u32[]{:S(2)}, u32[]{:S(2)}) collective-permute-start(bf16[512,3072]{1,0:T(8,128)(2,1)S(1)} %pad_maximum_fusion.10), channel_id=1, source_target_pairs={{0,2},{1,3},{2,0},{3,1},{4,6},{5,7},{6,4},{7,5},{8,10},{9,11},{10,... | collective-permute-start | bytes 9437192 | tf_op jit(solution)/shard_map/ppermute | solution.py:18
  2325.1 268.2 %collective-permute-start.3 = (bf16[512,3072]{1,0:T(8,128)(2,1)S(1)}, bf16[512,3072]{1,0:T(8,128)(2,1)S(1)}, u32[]{:S(2)}, u32[]{:S(2)}) collective-permute-start(bf16[512,3072]{1,0:T(8,128)(2,1)S(1)} %pad_maximum_fusion.11), channel_id=1, source_target_pairs={{0,2},{1,3},{2,0},{3,1},{4,6},{5,7},{6,4},{7,5},{8,10},{9,11},{10,... | collective-permute-start | bytes 9437192 | tf_op jit(solution)/shard_map/ppermute | solution.py:18
  2647.2 584.9 %reduce-scatter.33.cloned.1.call-start = ((), (), s32[]{:S(2)}) async-start(), calls=%async_computation.30 | async-start | bytes 28311552 | tf_op jit(solution)/shard_map/reduce_scatter | solution.py:318
  2685.6 554.6 %reduce-scatter.23.cloned.1.call-start = ((), (), s32[]{:S(2)}) async-start(), calls=%async_computation.25 | async-start | bytes 7864320 | tf_op jit(solution)/shard_map/reduce_scatter | solution.py:305
  2954.7 333.8 %reduce-scatter.27.cloned.1.call-start = ((), (), s32[]{:S(2)}) async-start(), calls=%async_computation.27 | async-start | bytes 7864320 | tf_op jit(solution)/shard_map/reduce_scatter | solution.py:305
  3176.7 217.6 %reduce-scatter.29.cloned.1.call-start = ((), (), s32[]{:S(2)}) async-start(), calls=%async_computation.28 | async-start | bytes 15925248 | tf_op jit(solution)/shard_map/reduce_scatter | solution.py:312
  (93 other events, 2518.1 us)
Sparse Core Ops, SparseCore 0:
  14.3 118.2 all-gather.12
  135.0 79.7 all-gather.14
  216.7 38.9 all-gather.16
  257.6 115.3 all-gather.24
  375.2 210.0 reduce-scatter.12
  587.5 212.8 reduce-scatter.16
  802.9 126.3 all-gather.20
  931.5 115.3 all-gather.18
  1049.0 113.5 all-gather.28
  1164.4 70.3 all-gather.22
  1294.1 211.8 reduce-scatter.20
  1512.1 116.3 all-gather.26
  1630.1 113.5 all-gather.30
  1803.2 210.0 reduce-scatter.24
  2016.0 111.7 reduce-scatter.14
  2130.6 111.2 reduce-scatter.18
  2245.3 92.9 reduce-scatter.34
  2647.3 54.5 reduce-scatter.30
  2706.0 156.8 reduce-scatter.32
  2954.8 111.3 reduce-scatter.22
  3176.9 111.5 reduce-scatter.26
  3292.5 101.8 reduce-scatter.28
